TPU v7x, 32 devices: a whole 2x2x4 slice. The times are simulated.
32 devices in a mesh: dp: 8 (over y, x, core), seq: 4 (over z).
Axes of the slice: x: 2, y: 2, z: 4, core: 2. Of those that a mesh axis runs over, the one named last changes fastest.
Arguments:
- inputs: bfloat16 [16, 576, 1152], P('dp', 'seq'), may hold values from -90 to 90
- cotangent: bfloat16 [16, 576, 1152], P('dp', 'seq'), may hold values from -6 to 6
- ln1_gain: bfloat16 [1152], P(('dp', 'seq')), may hold values from 0.099609375 to 1.8984375
- ln1_bias: bfloat16 [1152], P(('dp', 'seq')), may hold values from -3 to 3
- qkv_weight: bfloat16 [1152, 3456], P(('dp', 'seq')), may hold values from -0.1875 to 0.1875
- qv_bias: bfloat16 [2, 1152], P(None, ('dp', 'seq')), may hold values from -3 to 3
- out_weight: bfloat16 [1152, 1152], P(('dp', 'seq')), may hold values from -2.5 to 2.5
- out_bias: bfloat16 [1152], P(('dp', 'seq')), may hold values from -3 to 3
- ln2_gain: bfloat16 [1152], P(('dp', 'seq')), may hold values from 0.099609375 to 1.8984375
- ln2_bias: bfloat16 [1152], P(('dp', 'seq')), may hold values from -3 to 3
- up_weight: bfloat16 [1152, 4304], P(('dp', 'seq')), may hold values from -0.1875 to 0.1875
- up_bias: bfloat16 [4304], replicated, may hold values from -3 to 3
- down_weight: bfloat16 [4304, 1152], P(None, ('dp', 'seq')), may hold values from -0.09375 to 0.09375
- down_bias: bfloat16 [1152], P(('dp', 'seq')), may hold values from -3 to 3
Outputs:
- output: bfloat16 [16, 576, 1152], P('dp', 'seq')
- input_grad: bfloat16 [16, 576, 1152], P('dp', 'seq')
- ln1_gain_grad: float32 [1152], P(('dp', 'seq'))
- ln1_bias_grad: float32 [1152], P(('dp', 'seq'))
- qkv_weight_grad: float32 [1152, 3456], P(('dp', 'seq'))
- qv_bias_grad: float32 [2, 1152], P(None, ('dp', 'seq'))
- out_weight_grad: float32 [1152, 1152], P(('dp', 'seq'))
- out_bias_grad: float32 [1152], P(('dp', 'seq'))
- ln2_gain_grad: float32 [1152], P(('dp', 'seq'))
- ln2_bias_grad: float32 [1152], P(('dp', 'seq'))
- up_weight_grad: float32 [1152, 4304], P(('dp', 'seq'))
- up_bias_grad: float32 [4304], replicated
- down_weight_grad: float32 [4304, 1152], P(None, ('dp', 'seq'))
- down_bias_grad: float32 [1152], P(('dp', 'seq'))
All inputs are finite; a program needn't handle non-finite values.
Results may differ from a plain program's by a relative error of at most 0.012.
The roundings to bfloat16 on the way count: a program that leaves them out, or rounds other values in their place, can miss the bound.
Values may be sent and summed in bfloat16 or wider, within the bound.
No kernel may reach another device: no remote copies, remote signals or barrier semaphores. Data moves between devices by JAX's collectives and lax.ppermute only.
A program may use at most 320 MiB of HBM per device.

v0:
```python
import jax
import jax.numpy as jnp
from jax import lax
from jax.sharding import PartitionSpec as P

HEADS = 16
HEAD = 72
EPS = 1e-06
GELU_C = 0.7978845608028654
GELU_A = 0.044715


def layer_norm(values, gain_row, offset):
    average = jnp.mean(values, axis=-1, keepdims=True)
    centred = values - average
    variance = jnp.mean(centred * centred, axis=-1, keepdims=True)
    inverse = lax.rsqrt(variance + EPS)
    normed = centred * inverse
    return (normed, inverse, normed * gain_row + offset)


def norm_back(grad_normed, normed, inverse):
    mean_grad = jnp.mean(grad_normed, axis=-1, keepdims=True)
    mean_mixed = jnp.mean(grad_normed * normed, axis=-1, keepdims=True)
    return inverse * (grad_normed - mean_grad - normed * mean_mixed)


def gelu_parts(pre_act):
    inner_arg = GELU_C * (pre_act + GELU_A * pre_act * pre_act * pre_act)
    tangent = jnp.tanh(inner_arg)
    gelu_value = 0.5 * pre_act * (1.0 + tangent)
    slopes = 0.5 * (1.0 + tangent) + 0.5 * pre_act * (1.0 - tangent * tangent) * GELU_C * (
        1.0 + 3.0 * GELU_A * pre_act * pre_act
    )
    return (gelu_value, slopes)


def contract_rows(left, right):
    return lax.dot_general(
        left, right, (((0,), (0,)), ((), ())), preferred_element_type=jnp.float32
    )


def contract_cols(left, right):
    return lax.dot_general(
        left, right, (((1,), (1,)), ((), ())), preferred_element_type=jnp.float32
    )


def attend_block(queries, key_rows, value_rows, scaling, block_rows):
    length, head_count, head_width = queries.shape

    def one_block(block_index):
        query_block = lax.dynamic_slice_in_dim(queries, block_index * block_rows, block_rows, 0)
        scores = (
            jnp.einsum("qhd,khd->hqk", query_block, key_rows, preferred_element_type=jnp.float32)
            * scaling
        )
        row_top = jnp.max(scores, axis=-1, keepdims=True)
        log_total = row_top + jnp.log(jnp.sum(jnp.exp(scores - row_top), axis=-1, keepdims=True))
        weights_b = jnp.exp(scores - log_total).astype(jnp.bfloat16)
        attended = jnp.einsum(
            "hqk,khd->qhd", weights_b, value_rows, preferred_element_type=jnp.float32
        ).astype(jnp.bfloat16)
        return (attended, log_total[:, :, 0])

    attended, log_total = lax.map(one_block, jnp.arange(length // block_rows, dtype=jnp.int32))
    return (
        attended.reshape(length, head_count, head_width),
        jnp.moveaxis(log_total, 0, 1).reshape(head_count, length),
    )


def attend_back(
    queries, key_rows, value_rows, attended, log_total, grad_attended, scaling, block_rows
):
    length, head_count, head_width = queries.shape
    row_delta = jnp.sum(grad_attended.astype(jnp.float32) * attended.astype(jnp.float32), axis=-1)

    def one_block(running, block_index):
        key_grad, value_grad = running
        row_start = block_index * block_rows
        query_block = lax.dynamic_slice_in_dim(queries, row_start, block_rows, 0)
        grad_block = lax.dynamic_slice_in_dim(grad_attended, row_start, block_rows, 0)
        log_block = lax.dynamic_slice_in_dim(log_total, row_start, block_rows, 1)
        delta_block = lax.dynamic_slice_in_dim(row_delta, row_start, block_rows, 0)
        scores = (
            jnp.einsum("qhd,khd->hqk", query_block, key_rows, preferred_element_type=jnp.float32)
            * scaling
        )
        probabilities = jnp.exp(scores - log_block[:, :, None])
        value_grad = value_grad + jnp.einsum(
            "hqk,qhd->khd",
            probabilities.astype(jnp.bfloat16),
            grad_block,
            preferred_element_type=jnp.float32,
        )
        prob_grad = jnp.einsum(
            "qhd,khd->hqk", grad_block, value_rows, preferred_element_type=jnp.float32
        )
        score_grad = (
            probabilities * (prob_grad - jnp.transpose(delta_block)[:, :, None]) * scaling
        ).astype(jnp.bfloat16)
        query_grad = jnp.einsum(
            "hqk,khd->qhd", score_grad, key_rows, preferred_element_type=jnp.float32
        )
        key_grad = key_grad + jnp.einsum(
            "hqk,qhd->khd", score_grad, query_block, preferred_element_type=jnp.float32
        )
        return ((key_grad, value_grad), query_grad)

    zero_grad = jnp.zeros((length, head_count, head_width), jnp.float32)
    (key_grad, value_grad), query_grad = lax.scan(
        one_block, (zero_grad, zero_grad), jnp.arange(length // block_rows, dtype=jnp.int32)
    )
    return (query_grad.reshape(length, head_count, head_width), key_grad, value_grad)


def local(
    inputs,
    cotangent,
    ln1_gain,
    ln1_bias,
    qkv_weight,
    qv_bias,
    out_weight,
    out_bias,
    ln2_gain,
    ln2_bias,
    up_weight,
    up_bias,
    down_weight,
    down_bias,
):
    images, tok_rows, model_width = inputs.shape
    groups = lax.axis_size("seq")
    head_share = HEADS // groups
    length = tok_rows * groups
    row_count = images * tok_rows
    scaling = HEAD ** (-0.5)
    block_rows = min(576, length)
    attn_set = (
        lax.all_gather(ln1_gain, ("dp", "seq"), axis=0, tiled=True),
        lax.all_gather(ln1_bias, ("dp", "seq"), axis=0, tiled=True),
        lax.all_gather(qkv_weight, ("dp", "seq"), axis=0, tiled=True),
        lax.all_gather(qv_bias, ("dp", "seq"), axis=1, tiled=True),
        lax.all_gather(out_weight, ("dp", "seq"), axis=0, tiled=True),
        lax.all_gather(out_bias, ("dp", "seq"), axis=0, tiled=True),
    )
    gain_one, shift_one, qkv_full, qv_full, out_full, out_bias_full = attn_set
    gain_one_f = gain_one.astype(jnp.float32)
    input_f = inputs.reshape(row_count, model_width).astype(jnp.float32)
    normed1, inverse1, shifted1 = layer_norm(input_f, gain_one_f, shift_one.astype(jnp.float32))
    attn_input = shifted1.astype(jnp.bfloat16)
    bias_full = jnp.concatenate(
        [
            qv_full[0].astype(jnp.float32),
            jnp.zeros((model_width,), jnp.float32),
            qv_full[1].astype(jnp.float32),
        ]
    )
    projected = (
        jnp.dot(attn_input, qkv_full, preferred_element_type=jnp.float32) + bias_full
    ).astype(jnp.bfloat16)
    projected = projected.reshape(images, tok_rows, 3, model_width)
    by_heads = lax.all_to_all(projected, "seq", split_axis=3, concat_axis=1, tiled=True)

    def attend_one(one_image):
        queries = one_image[:, 0].reshape(length, head_share, HEAD)
        key_rows = one_image[:, 1].reshape(length, head_share, HEAD)
        value_rows = one_image[:, 2].reshape(length, head_share, HEAD)
        return attend_block(queries, key_rows, value_rows, scaling, block_rows)

    attended_heads, log_totals = lax.map(attend_one, by_heads)
    attended_tok = lax.all_to_all(
        attended_heads.reshape(images, length, head_share * HEAD),
        "seq",
        split_axis=1,
        concat_axis=2,
        tiled=True,
    )
    attended_flat = attended_tok.reshape(row_count, model_width)
    hidden = (
        input_f
        + jnp.dot(attended_flat, out_full, preferred_element_type=jnp.float32)
        + out_bias_full.astype(jnp.float32)
    )
    mlp_set = (
        lax.all_gather(ln2_gain, ("dp", "seq"), axis=0, tiled=True),
        lax.all_gather(ln2_bias, ("dp", "seq"), axis=0, tiled=True),
        lax.all_gather(up_weight, ("dp", "seq"), axis=0, tiled=True),
        lax.all_gather(down_weight, ("dp", "seq"), axis=1, tiled=True),
        lax.all_gather(down_bias, ("dp", "seq"), axis=0, tiled=True),
    )
    gain_two, shift_two, up_full, down_full, down_bias_full = mlp_set
    normed2, inverse2, shifted2 = layer_norm(
        hidden, gain_two.astype(jnp.float32), shift_two.astype(jnp.float32)
    )
    mlp_input = shifted2.astype(jnp.bfloat16)
    pre_act = jnp.dot(mlp_input, up_full, preferred_element_type=jnp.float32) + up_bias.astype(
        jnp.float32
    )
    gelu_value, slopes = gelu_parts(pre_act)
    gelu_out = gelu_value.astype(jnp.bfloat16)
    result = (
        hidden
        + jnp.dot(gelu_out, down_full, preferred_element_type=jnp.float32)
        + down_bias_full.astype(jnp.float32)
    ).astype(jnp.bfloat16)
    gain_two_back, up_back, down_back = (
        lax.all_gather(ln2_gain, ("dp", "seq"), axis=0, tiled=True),
        lax.all_gather(up_weight, ("dp", "seq"), axis=0, tiled=True),
        lax.all_gather(down_weight, ("dp", "seq"), axis=1, tiled=True),
    )
    grad_rows = cotangent.reshape(row_count, model_width)
    grad_f = grad_rows.astype(jnp.float32)
    down_bias_grad = jnp.sum(grad_f, axis=0)
    down_weight_grad = contract_rows(gelu_out, grad_rows)
    gelu_grad = contract_cols(grad_rows, down_back)
    pre_grad = (gelu_grad * slopes).astype(jnp.bfloat16)
    up_weight_grad = contract_rows(mlp_input, pre_grad)
    up_bias_part = jnp.sum(pre_grad.astype(jnp.float32), axis=0)
    mlp_in_grad = contract_cols(pre_grad, up_back)
    ln2_gain_grad = jnp.sum(mlp_in_grad * normed2, axis=0)
    ln2_bias_grad = jnp.sum(mlp_in_grad, axis=0)
    hidden_grad = grad_f + norm_back(
        mlp_in_grad * gain_two_back.astype(jnp.float32), normed2, inverse2
    )
    mlp_owned = (
        lax.psum_scatter(ln2_gain_grad, ("dp", "seq"), scatter_dimension=0, tiled=True),
        lax.psum_scatter(ln2_bias_grad, ("dp", "seq"), scatter_dimension=0, tiled=True),
        lax.psum_scatter(up_weight_grad, ("dp", "seq"), scatter_dimension=0, tiled=True),
        lax.psum_scatter(down_weight_grad, ("dp", "seq"), scatter_dimension=1, tiled=True),
        lax.psum_scatter(down_bias_grad, ("dp", "seq"), scatter_dimension=0, tiled=True),
    )
    up_bias_total = lax.psum(up_bias_part, ("dp", "seq"))
    gain_one_back, qkv_back, out_back = (
        lax.all_gather(ln1_gain, ("dp", "seq"), axis=0, tiled=True),
        lax.all_gather(qkv_weight, ("dp", "seq"), axis=0, tiled=True),
        lax.all_gather(out_weight, ("dp", "seq"), axis=0, tiled=True),
    )
    out_bias_grad = jnp.sum(hidden_grad, axis=0)
    hidden_grad_b = hidden_grad.astype(jnp.bfloat16)
    out_weight_grad = contract_rows(attended_flat, hidden_grad_b)
    attended_grad = (
        contract_cols(hidden_grad_b, out_back)
        .astype(jnp.bfloat16)
        .reshape(images, tok_rows, model_width)
    )
    grad_heads = lax.all_to_all(attended_grad, "seq", split_axis=2, concat_axis=1, tiled=True)

    def attend_back_one(pieces):
        heads_in, attended_in, logs_in, grads_in = pieces
        queries = heads_in[:, 0].reshape(length, head_share, HEAD)
        key_rows = heads_in[:, 1].reshape(length, head_share, HEAD)
        value_rows = heads_in[:, 2].reshape(length, head_share, HEAD)
        grads_split = grads_in.reshape(length, head_share, HEAD)
        query_grad, key_grad, value_grad = attend_back(
            queries, key_rows, value_rows, attended_in, logs_in, grads_split, scaling, block_rows
        )
        flat_width = head_share * HEAD
        return jnp.stack(
            [
                query_grad.reshape(length, flat_width),
                key_grad.reshape(length, flat_width),
                value_grad.reshape(length, flat_width),
            ],
            axis=1,
        ).astype(jnp.bfloat16)

    stacked_grads = lax.map(attend_back_one, (by_heads, attended_heads, log_totals, grad_heads))
    projected_grad = lax.all_to_all(
        stacked_grads, "seq", split_axis=1, concat_axis=3, tiled=True
    ).reshape(row_count, 3 * model_width)
    qkv_weight_grad = contract_rows(attn_input, projected_grad)
    projected_f = projected_grad.astype(jnp.float32)
    qv_bias_grad = jnp.stack(
        [
            jnp.sum(projected_f[:, :model_width], axis=0),
            jnp.sum(projected_f[:, 2 * model_width :], axis=0),
        ]
    )
    attn_in_grad = contract_cols(projected_grad, qkv_back)
    ln1_gain_grad = jnp.sum(attn_in_grad * normed1, axis=0)
    ln1_bias_grad = jnp.sum(attn_in_grad, axis=0)
    input_grad = (
        hidden_grad + norm_back(attn_in_grad * gain_one_back.astype(jnp.float32), normed1, inverse1)
    ).astype(jnp.bfloat16)
    attn_owned = (
        lax.psum_scatter(ln1_gain_grad, ("dp", "seq"), scatter_dimension=0, tiled=True),
        lax.psum_scatter(ln1_bias_grad, ("dp", "seq"), scatter_dimension=0, tiled=True),
        lax.psum_scatter(qkv_weight_grad, ("dp", "seq"), scatter_dimension=0, tiled=True),
        lax.psum_scatter(qv_bias_grad, ("dp", "seq"), scatter_dimension=1, tiled=True),
        lax.psum_scatter(out_weight_grad, ("dp", "seq"), scatter_dimension=0, tiled=True),
        lax.psum_scatter(out_bias_grad, ("dp", "seq"), scatter_dimension=0, tiled=True),
    )
    owned_all = attn_owned + mlp_owned
    return (
        result.reshape(images, tok_rows, model_width),
        input_grad.reshape(images, tok_rows, model_width),
        owned_all[0],
        owned_all[1],
        owned_all[2],
        owned_all[3],
        owned_all[4],
        owned_all[5],
        owned_all[6],
        owned_all[7],
        owned_all[8],
        up_bias_total,
        owned_all[9],
        owned_all[10],
    )


def solution(mesh):
    in_specs = (
        P("dp", "seq", None),
        P("dp", "seq", None),
        P(("dp", "seq")),
        P(("dp", "seq")),
        P(("dp", "seq"), None),
        P(None, ("dp", "seq")),
        P(("dp", "seq"), None),
        P(("dp", "seq")),
        P(("dp", "seq")),
        P(("dp", "seq")),
        P(("dp", "seq"), None),
        P(),
        P(None, ("dp", "seq")),
        P(("dp", "seq")),
    )
    out_specs = (
        P("dp", "seq", None),
        P("dp", "seq", None),
        P(("dp", "seq")),
        P(("dp", "seq")),
        P(("dp", "seq"), None),
        P(None, ("dp", "seq")),
        P(("dp", "seq"), None),
        P(("dp", "seq")),
        P(("dp", "seq")),
        P(("dp", "seq")),
        P(("dp", "seq"), None),
        P(),
        P(None, ("dp", "seq")),
        P(("dp", "seq")),
    )
    return jax.shard_map(local, mesh=mesh, in_specs=in_specs, out_specs=out_specs, check_vma=False)
```

profile of v0, /device:TPU:19, one launch (start us, length us, event | category | flops | bytes accessed | tf_op | source)
XLA Modules:
  0.0 2467.8 jit_solution(2320902800671834990)
XLA Ops:
  17.9 41.7 %all-reduce.22 = (bf16[1152]{0:T(1024)(128)(2,1)S(1)}, bf16[1152]{0:T(1024)(128)(2,1)S(1)}, bf16[1152]{0:T(1024)(128)(2,1)}, bf16[1152]{0:T(1024)(128)(2,1)}, bf...) all-reduce(bf16[1152]{0:T(1024)(128)(2,1)S(1)} %dynamic-update-slic, ...), channel_id=1, replica_groups=mesh['dp'=8,'seq'=4] {'dp','seq'}, use_global_device_ids=true, to_apply=%add.1 | all-reduce | flops 6912 | bytes 27648
  59.7 62.3 %all-gather.1 = bf16[32,36,2]{1,2,0:T(2,128)(2,1)S(1)} all-gather(bf16[1,36,2]{1,2,0:T(2,128)(2,1)} %bitcast.199), channel_id=1, replica_groups=mesh['dp'=8,'seq'=4] {'dp','seq'}, dimensions={0}, use_global_device_ids=true | all-gather | bytes 4752 | tf_op jit(solution)/shard_map/all_gather | solution.py:146
  123.6 12.4 reshape.265
  136.0 6.5 fusion.22
  142.5 2.9 reshape.240
  145.4 12.5 copy.73
  157.9 5.7 all-to-all-start
  163.6 110.8 %all-to-all-done = bf16[2,144,3,1152]{1,0,2,3:T(2,128)(2,1)} async-done(((bf16[2,144,3,1152]{1,0,2,3:T(2,128)(2,1)}), bf16[2,144,3,1152]{1,0,2,3:T(2,128)(2,1)}, u32[]{:S(2)}, u32[]{:S(2)}) %all-to-all-start) | async-done | bytes 1990688 | tf_op jit(solution)/shard_map/all_to_all | solution.py:166
  274.4 12.5 copy.89
  286.9 3.7 copy.75
  290.6 3.5 copy.76
  294.1 9.9 while.18
  304.1 3.2 copy.77
  307.2 7.6 all-to-all-start.1
  322.1 5.2 reshape.269
  327.2 14.6 reshape.271
  341.8 51.9 %all-gather.16.cloned.1.call-done = bf16[32,36,4304]{2,1,0:T(8,128)(2,1)} async-done(((bf16[1,36,4304]{2,1,0:T(8,128)(2,1)}), bf16[32,36,4304]{2,1,0:T(8,128)(2,1)}) %all-gather.16.cloned.1.call-update) | async-done | bytes 9916432 | tf_op jit(solution)/shard_map/all_gather | solution.py:192
  393.7 14.6 reshape.273
  410.9 2.5 reshape.242
  413.4 3.1 fusion.46
  416.9 6.7 convolution_add_fusion
  423.7 9.9 fusion.40
  433.6 6.7 convert_reduce_fusion
  440.3 9.0 multiply_reduce_fusion.1
  453.0 4.0 copy.80
  457.1 5.0 all-to-all-start.2
  462.1 494.5 %fusion.3 = f32[4304,40]{0,1:T(8,128)} fusion(f32[4304,1152]{0,1:T(8,128)} %fusion.40), kind=kCustom, calls=%all-reduce-scatter.3 | all-reduce-scatter fusion | flops 5509121 | bytes 20521472
  956.6 4.4 collective-permute-start.22
  961.0 4.3 collective-permute-start.21
  967.2 4.9 copy.90
  976.6 23.9 while.19
  981.9 2.3 multiply_convert_fusion.5
  993.9 2.3 multiply_convert_fusion.5
  1000.5 7.1 copy.85
  1007.6 7.3 all-to-all-start.3
  1014.9 11.3 fusion.39
  1026.2 9.9 fusion.30
  1039.0 4.0 fusion.34
  1043.6 15.5 concatenate.15
  1060.0 18.3 all-to-all-done.3
  1080.4 2.5 copy.87
  1083.0 3.8 reshape.246
  1086.8 7.9 fusion.48
  1094.7 1056.8 %fusion.42 = (f32[48,3456]{1,0:T(8,128)S(1)}, f32[48,1152]{1,0:T(8,128)S(1)}, f32[40,4304]{1,0:T(8,128)}) fusion(f32[1152,3456]{1,0:T(8,128)} %fusion.48, f32[1152,1152]{1,0:T(8,128)} %fusion.34, f32[1152,4304]{1,0:T(8,128)} %fusion.39), kind=kCustom, calls=%all-reduce-scatter.4 | all-reduce-scatter fusion | flops 12587010 | bytes 42639872
  2151.5 4.2 collective-permute-start.14
  2155.8 8.2 fusion.41
  2164.3 4.3 collective-permute-start.13
  2175.5 27.1 %collective-permute-done.15 = f32[36,1152]{1,0:T(8,128)S(1)} collective-permute-done((f32[36,1152]{1,0:T(8,128)S(1)}, f32[36,1152]{1,0:T(8,128)S(1)}, u32[]{:S(2)}, u32[]{:S(2)}) %collective-permute-start.15) | collective-permute-done | bytes 165920
  2202.5 3.6 collective-permute-start.5
  2209.4 61.9 %all-reduce.21 = (f32[1152]{0:T(1024)}, f32[1152]{0:T(1024)}, f32[2,1152]{1,0:T(2,128)}, f32[1152]{0:T(1024)}, f32[1152]{0:T(1024)}, /*index=5*/f32[1152]{0:T(1024)}, f32[4304]{0:T(1024)}, f32[1152]{0:T(1024)}) all-reduce(f32[1152]{0:T(1024)} %get-tuple-element.169, ...), channel_id=2, replica_groups=mesh['dp'=8,'seq'=4] {'dp','seq'}, use_global_device_ids=true, to_apply=%region_16.17.clone | all-reduce | flops 13520 | bytes 108160
  2271.4 5.5 collective-permute-start.11
  2279.7 6.9 collective-permute-start.9
  2286.6 4.9 collective-permute-start.8
  2292.2 7.6 collective-permute-done.9
  2302.1 3.4 collective-permute-start.3
  2318.0 8.2 collective-permute-start.1
  2328.1 2.7 add_convert_fusion.1
  2330.8 8.7 concatenate.13
  2341.5 2.5 collective-permute-start.17
  2344.0 2.5 collective-permute-start.16
  2347.2 31.3 %collective-permute-done.1 = f32[48,3456]{1,0:T(8,128)} collective-permute-done((f32[48,3456]{1,0:T(8,128)S(1)}, f32[48,3456]{1,0:T(8,128)}, u32[]{:S(2)}, u32[]{:S(2)}) %collective-permute-start.1) | collective-permute-done | bytes 663584
  2380.7 26.2 %collective-permute-done = f32[48,3456]{1,0:T(8,128)} collective-permute-done((f32[48,3456]{1,0:T(8,128)S(1)}, f32[48,3456]{1,0:T(8,128)}, u32[]{:S(2)}, u32[]{:S(2)}) %collective-permute-start) | collective-permute-done | bytes 663584
  2406.9 36.8 %concatenate.12 = f32[420,3456]{1,0:T(8,128)} concatenate(f32[36,3456]{1,0:T(8,128)} %collective-permute-done.7, f32[48,3456]{1,0:T(8,128)} %copy-done.17, f32[48,3456]{1,0:T(8,128)} %collective-permute-done.5, f32[48,3456]{1,0:T(8,128)} %collective-permute-done.4, f32[48,3456]{1,0:T(8,128)} %collective-permute-done.3, f32[48,3456]{1,0:T(8,128)} %collective-permute-done.2, ...), dimensions={0} | concatenate | bytes 11612160
  2445.6 14.5 concatenate.14
  (243 shorter events, 105.9 us)
Async XLA Ops:
  7.2 115.0 %copy-start = (bf16[2,144,1152]{2,1,0:T(8,128)(2,1)S(1)}, bf16[2,144,1152]{2,1,0:T(8,128)(2,1)}, u32[]{:S(2)}) copy-start(bf16[2,144,1152]{2,1,0:T(8,128)(2,1)} %param.18) | copy-start | bytes 1990660
  7.2 116.4 %all-gather.10.cloned.1.call-start = ((), (), s32[]{:S(2)}) async-start(), calls=%async_computation.4 | async-start | bytes 9123840 | tf_op jit(solution)/shard_map/all_gather | solution.py:145
  7.9 314.2 %all-gather.12.cloned.1.call-start = ((), (), s32[]{:S(2)}) async-start(), calls=%async_computation.5 | async-start | bytes 3041280 | tf_op jit(solution)/shard_map/all_gather | solution.py:147
  8.7 318.6 %all-gather.14.cloned.1.call-start = ((), (), s32[]{:S(2)}) async-start(), calls=%async_computation.6 | async-start | bytes 11489280 | tf_op jit(solution)/shard_map/all_gather | solution.py:191
  9.4 384.3 %all-gather.16.cloned.1.call-start = ((), (), s32[]{:S(2)}) async-start(), calls=%async_computation.7 | async-start | bytes 11489280 | tf_op jit(solution)/shard_map/all_gather | solution.py:192
  11.3 112.3 %copy-start.33 = (f32[2,144]{1,0:T(2,128)}, f32[2,144]{1,0:T(2,128)S(1)}, u32[]{:S(2)}) copy-start(f32[2,144]{1,0:T(2,128)S(1)} %broadcast_multiply_fusion.5) | copy-start | bytes 3460
  11.3 124.6 %copy-start.36 = (f32[288]{0:T(512)}, f32[288]{0:T(512)S(1)}, u32[]{:S(2)}) copy-start(f32[288]{0:T(512)S(1)} %div.27) | copy-start | bytes 3460
  12.8 110.8 %copy-start.35 = (f32[2,144]{1,0:T(2,128)}, f32[2,144]{1,0:T(2,128)S(1)}, u32[]{:S(2)}) copy-start(f32[2,144]{1,0:T(2,128)S(1)} %add_rsqrt_fusion.1) | copy-start | bytes 3460
  12.9 123.1 %copy-start.38 = (f32[288]{0:T(512)}, f32[288]{0:T(512)S(1)}, u32[]{:S(2)}) copy-start(f32[288]{0:T(512)S(1)} %rsqrt.21) | copy-start | bytes 3460
  59.7 76.3 %copy-start.32 = (f32[1152]{0:T(1024)}, f32[1152]{0:T(1024)S(1)}, u32[]{:S(2)}) copy-start(f32[1152]{0:T(1024)S(1)} %convert_element_type.138) | copy-start | bytes 13828
  59.7 76.3 %copy-start.26 = (f32[1152]{0:T(1024)}, f32[1152]{0:T(1024)S(1)}, u32[]{:S(2)}) copy-start(f32[1152]{0:T(1024)S(1)} %convert_element_type.137) | copy-start | bytes 13828
  157.9 116.5 %all-to-all-start = ((bf16[2,144,3,1152]{1,0,2,3:T(2,128)(2,1)}), bf16[2,144,3,1152]{1,0,2,3:T(2,128)(2,1)}, u32[]{:S(2)}, u32[]{:S(2)}) async-start(bf16[2,144,3,1152]{1,0,2,3:T(2,128)(2,1)} %copy.73), calls=%async_computation | async-start | bytes 7077888 | tf_op jit(solution)/shard_map/all_to_all | solution.py:166
  304.1 15.4 copy-start.9
  307.2 101.1 %all-to-all-start.1 = ((bf16[2,576,288]{2,0,1:T(2,128)(2,1)}), bf16[2,576,288]{2,0,1:T(2,128)(2,1)}, u32[]{:S(2)}, u32[]{:S(2)}) async-start(bf16[2,576,288]{2,0,1:T(2,128)(2,1)} %copy.77), calls=%async_computation.1 | async-start | bytes 1769472 | tf_op jit(solution)/shard_map/all_to_all | solution.py:175
  416.5 32.7 %copy-start.4 = (f32[288,1152]{1,0:T(8,128)}, f32[288,1152]{1,0:T(8,128)S(1)}, u32[]{:S(2)}) copy-start(f32[288,1152]{1,0:T(8,128)S(1)} %get-tuple-element.227) | copy-start | bytes 3981316
  416.6 32.7 %copy-start.24 = (f32[288]{0:T(512)}, f32[288]{0:T(512)S(1)}, u32[]{:S(2)}) copy-start(f32[288]{0:T(512)S(1)} %broadcast_multiply_fusion.4) | copy-start | bytes 3460
  416.9 32.4 %copy-start.29 = (f32[288]{0:T(512)}, f32[288]{0:T(512)S(1)}, u32[]{:S(2)}) copy-start(f32[288]{0:T(512)S(1)} %add_rsqrt_fusion) | copy-start | bytes 3460
  416.9 16.7 slice-start
  416.9 16.7 slice-start.1
  423.7 9.9 copy-start.6
  423.7 9.9 slice-start.2
  440.3 9.0 copy-start.10
  450.5 588.5 %copy-start.2 = (f32[288,1152]{1,0:T(8,128)}, f32[288,1152]{1,0:T(8,128)S(1)}, u32[]{:S(2)}) copy-start(f32[288,1152]{1,0:T(8,128)S(1)} %get-tuple-element.217) | copy-start | bytes 3981316
  457.1 510.2 %all-to-all-start.2 = ((bf16[2,144,1152]{1,0,2:T(2,128)(2,1)}), bf16[2,144,1152]{1,0,2:T(2,128)(2,1)}, u32[]{:S(2)}, u32[]{:S(2)}) async-start(bf16[2,144,1152]{1,0,2:T(2,128)(2,1)} %copy.80), calls=%async_computation.2 | async-start | bytes 2359296 | tf_op jit(solution)/shard_map/all_to_all | solution.py:250
  956.6 86.3 %collective-permute-start.22 = (f32[4304,40]{0,1:T(8,128)}, f32[4304,40]{0,1:T(8,128)}, u32[]{:S(2)}, u32[]{:S(2)}) collective-permute-start(f32[4304,40]{0,1:T(8,128)} %fusion.3), channel_id=1, source_target_pairs={{0,3},{1,4},{2,5},{3,6},{4,7},{5,8},{6,9},{7,10},{8,11},{9,12},{10... | collective-permute-start | bytes 2065928
  961.0 81.9 %collective-permute-start.21 = (f32[4304,40]{0,1:T(8,128)}, f32[4304,40]{0,1:T(8,128)}, u32[]{:S(2)}, u32[]{:S(2)}) collective-permute-start(f32[4304,40]{0,1:T(8,128)} %fusion.3), channel_id=1, source_target_pairs={{0,2},{1,3},{2,4},{3,5},{4,6},{5,7},{6,8},{7,9},{8,10},{9,11},{10,... | collective-permute-start | bytes 2065928
  965.3 78.3 %collective-permute-start.20 = (f32[4304,40]{0,1:T(8,128)}, f32[4304,40]{0,1:T(8,128)}, u32[]{:S(2)}, u32[]{:S(2)}) collective-permute-start(f32[4304,40]{0,1:T(8,128)} %fusion.3), channel_id=1, source_target_pairs={{0,1},{1,2},{2,3},{3,4},{4,5},{5,6},{6,7},{7,8},{8,9},{9,10},{10,1... | collective-permute-start | bytes 2065928
  1007.6 7.3 copy-start.30
  1007.6 70.7 %all-to-all-start.3 = ((bf16[2,576,3,288]{3,0,2,1:T(2,128)(2,1)}), bf16[2,576,3,288]{3,0,2,1:T(2,128)(2,1)}, u32[]{:S(2)}, u32[]{:S(2)}) async-start(bf16[2,576,3,288]{3,0,2,1:T(2,128)(2,1)} %copy.85), calls=%async_computation.3 | async-start | bytes 5308416 | tf_op jit(solution)/shard_map/all_to_all | solution.py:272
  1014.9 11.3 copy-start.40
  1026.2 12.7 copy-start.11
  1037.0 5.9 collective-permute-start.23
  1094.7 1061.1 %copy-start.1 = (bf16[2,144,1152]{2,1,0:T(8,128)(2,1)S(1)}, bf16[2,144,1152]{2,1,0:T(8,128)(2,1)}, u32[]{:S(2)}) copy-start(bf16[2,144,1152]{2,1,0:T(8,128)(2,1)} %param.18) | copy-start | bytes 1990660
  1094.7 1061.1 %copy-start.27 = (f32[1152]{0:T(1024)S(1)}, f32[1152]{0:T(1024)}, u32[]{:S(2)}) copy-start(f32[1152]{0:T(1024)} %copy-done.26) | copy-start | bytes 13828
  1094.7 1061.1 %copy-start.37 = (f32[288]{0:T(512)S(1)}, f32[288]{0:T(512)}, u32[]{:S(2)}) copy-start(f32[288]{0:T(512)} %copy-done.36) | copy-start | bytes 3460
  1094.7 1061.1 %copy-start.39 = (f32[288]{0:T(512)S(1)}, f32[288]{0:T(512)}, u32[]{:S(2)}) copy-start(f32[288]{0:T(512)} %copy-done.38) | copy-start | bytes 3460
  2151.5 54.6 %collective-permute-start.14 = (f32[48,1152]{1,0:T(8,128)S(1)}, f32[48,1152]{1,0:T(8,128)S(1)}, u32[]{:S(2)}, u32[]{:S(2)}) collective-permute-start(f32[48,1152]{1,0:T(8,128)S(1)} %get-tuple-element.212), channel_id=1, source_target_pairs={{0,7},{1,8},{2,9},{3,10},{4,11},{5,12},{6,13},{7,14},{8,15},{9,16}... | collective-permute-start | bytes 663560
  2164.3 45.2 %copy-start.31 = (f32[1152]{0:T(1024)S(1)}, f32[1152]{0:T(1024)}, u32[]{:S(2)}) copy-start(f32[1152]{0:T(1024)} %convert_reduce_fusion.1) | copy-start | bytes 13828
  2164.3 163.9 %copy-start.3 = (f32[288,1152]{1,0:T(8,128)S(1)}, f32[288,1152]{1,0:T(8,128)}, u32[]{:S(2)}) copy-start(f32[288,1152]{1,0:T(8,128)} %copy-done.2) | copy-start | bytes 3981316
  2164.3 107.1 %collective-permute-start.13 = (f32[48,1152]{1,0:T(8,128)S(1)}, f32[48,1152]{1,0:T(8,128)}, u32[]{:S(2)}, u32[]{:S(2)}) collective-permute-start(f32[48,1152]{1,0:T(8,128)S(1)} %get-tuple-element.212), channel_id=1, source_target_pairs={{0,6},{1,7},{2,8},{3,9},{4,10},{5,11},{6,12},{7,13},{8,14},{9,15},... | collective-permute-start | bytes 663560
  2168.7 108.2 %collective-permute-start.12 = (f32[48,1152]{1,0:T(8,128)S(1)}, f32[48,1152]{1,0:T(8,128)}, u32[]{:S(2)}, u32[]{:S(2)}) collective-permute-start(f32[48,1152]{1,0:T(8,128)S(1)} %get-tuple-element.212), channel_id=1, source_target_pairs={{0,5},{1,6},{2,7},{3,8},{4,9},{5,10},{6,11},{7,12},{8,13},{9,14},{... | collective-permute-start | bytes 663560
  2171.5 146.5 %collective-permute-start.6 = (f32[48,3456]{1,0:T(8,128)S(1)}, f32[48,3456]{1,0:T(8,128)S(1)}, u32[]{:S(2)}, u32[]{:S(2)}) collective-permute-start(f32[48,3456]{1,0:T(8,128)S(1)} %get-tuple-element.211), channel_id=1, source_target_pairs={{0,7},{1,8},{2,9},{3,10},{4,11},{5,12},{6,13},{7,14},{8,15},{9,16}... | collective-permute-start | bytes 1990664
  2173.4 29.2 %collective-permute-start.15 = (f32[36,1152]{1,0:T(8,128)S(1)}, f32[36,1152]{1,0:T(8,128)S(1)}, u32[]{:S(2)}, u32[]{:S(2)}) collective-permute-start(f32[36,1152]{1,0:T(8,128)S(1)} %slice.45), channel_id=1, source_target_pairs={{0,8},{1,9},{2,10},{3,11},{4,12},{5,13},{6,14},{7,15},{8,16},{9,17... | collective-permute-start | bytes 497672
  2202.5 123.6 %collective-permute-start.5 = (f32[48,3456]{1,0:T(8,128)S(1)}, f32[48,3456]{1,0:T(8,128)}, u32[]{:S(2)}, u32[]{:S(2)}) collective-permute-start(f32[48,3456]{1,0:T(8,128)S(1)} %get-tuple-element.211), channel_id=1, source_target_pairs={{0,6},{1,7},{2,8},{3,9},{4,10},{5,11},{6,12},{7,13},{8,14},{9,15},... | collective-permute-start | bytes 1990664
  2206.9 98.6 %collective-permute-start.7 = (f32[36,3456]{1,0:T(8,128)}, f32[36,3456]{1,0:T(8,128)}, u32[]{:S(2)}, u32[]{:S(2)}) collective-permute-start(f32[36,3456]{1,0:T(8,128)} %slice.44), channel_id=1, source_target_pairs={{0,8},{1,9},{2,10},{3,11},{4,12},{5,13},{6,14},{7,15},{8,16},{9,17... | collective-permute-start | bytes 1493000
  2271.4 8.4 collective-permute-start.11
  2276.9 9.8 collective-permute-start.10
  2279.7 46.5 %copy-start.19 = (f32[48,1152]{1,0:T(8,128)}, f32[48,1152]{1,0:T(8,128)S(1)}, u32[]{:S(2)}) copy-start(f32[48,1152]{1,0:T(8,128)S(1)} %collective-permute-done.11) | copy-start | bytes 663556
  2279.7 20.1 collective-permute-start.9
  2286.6 41.5 %copy-start.20 = (f32[48,1152]{1,0:T(8,128)}, f32[48,1152]{1,0:T(8,128)S(1)}, u32[]{:S(2)}) copy-start(f32[48,1152]{1,0:T(8,128)S(1)} %collective-permute-done.10) | copy-start | bytes 663556
  2286.6 15.5 collective-permute-start.8
  2299.8 28.3 %copy-start.21 = (f32[48,1152]{1,0:T(8,128)}, f32[48,1152]{1,0:T(8,128)S(1)}, u32[]{:S(2)}) copy-start(f32[48,1152]{1,0:T(8,128)S(1)} %collective-permute-done.9) | copy-start | bytes 663556
  2299.8 39.7 %collective-permute-start.4 = (f32[48,3456]{1,0:T(8,128)S(1)}, f32[48,3456]{1,0:T(8,128)}, u32[]{:S(2)}, u32[]{:S(2)}) collective-permute-start(f32[48,3456]{1,0:T(8,128)S(1)} %get-tuple-element.211), channel_id=1, source_target_pairs={{0,5},{1,6},{2,7},{3,8},{4,9},{5,10},{6,11},{7,12},{8,13},{9,14},{... | collective-permute-start | bytes 1990664
  2302.1 26.0 %copy-start.22 = (f32[48,1152]{1,0:T(8,128)}, f32[48,1152]{1,0:T(8,128)S(1)}, u32[]{:S(2)}) copy-start(f32[48,1152]{1,0:T(8,128)S(1)} %collective-permute-done.8) | copy-start | bytes 663556
  2302.1 39.4 %collective-permute-start.3 = (f32[48,3456]{1,0:T(8,128)S(1)}, f32[48,3456]{1,0:T(8,128)}, u32[]{:S(2)}, u32[]{:S(2)}) collective-permute-start(f32[48,3456]{1,0:T(8,128)S(1)} %get-tuple-element.211), channel_id=1, source_target_pairs={{0,4},{1,5},{2,6},{3,7},{4,8},{5,9},{6,10},{7,11},{8,12},{9,13},{1... | collective-permute-start | bytes 1990664
  2305.5 38.5 %collective-permute-start.2 = (f32[48,3456]{1,0:T(8,128)S(1)}, f32[48,3456]{1,0:T(8,128)}, u32[]{:S(2)}, u32[]{:S(2)}) collective-permute-start(f32[48,3456]{1,0:T(8,128)S(1)} %get-tuple-element.211), channel_id=1, source_target_pairs={{0,3},{1,4},{2,5},{3,6},{4,7},{5,8},{6,9},{7,10},{8,11},{9,12},{10... | collective-permute-start | bytes 1990664
  2318.0 10.2 copy-start.17
  2318.0 60.5 %collective-permute-start.1 = (f32[48,3456]{1,0:T(8,128)S(1)}, f32[48,3456]{1,0:T(8,128)}, u32[]{:S(2)}, u32[]{:S(2)}) collective-permute-start(f32[48,3456]{1,0:T(8,128)S(1)} %get-tuple-element.211), channel_id=1, source_target_pairs={{0,2},{1,3},{2,4},{3,5},{4,6},{5,7},{6,8},{7,9},{8,10},{9,11},{10,... | collective-permute-start | bytes 1990664
  2326.2 80.8 %collective-permute-start = (f32[48,3456]{1,0:T(8,128)S(1)}, f32[48,3456]{1,0:T(8,128)}, u32[]{:S(2)}, u32[]{:S(2)}) collective-permute-start(f32[48,3456]{1,0:T(8,128)S(1)} %get-tuple-element.211), channel_id=1, source_target_pairs={{0,1},{1,2},{2,3},{3,4},{4,5},{5,6},{6,7},{7,8},{8,9},{9,10},{10,1... | collective-permute-start | bytes 1990664
  2330.8 8.7 copy-start.13
  2339.5 106.1 %collective-permute-start.18 = (f32[40,4304]{1,0:T(8,128)S(1)}, f32[40,4304]{1,0:T(8,128)}, u32[]{:S(2)}, u32[]{:S(2)}) collective-permute-start(f32[40,4304]{1,0:T(8,128)S(1)} %copy-done.13), channel_id=1, source_target_pairs={{0,3},{1,4},{2,5},{3,6},{4,7},{5,8},{6,9},{7,10},{8,11},{9,12},{10... | collective-permute-start | bytes 2065928
  2341.5 104.1 %collective-permute-start.17 = (f32[40,4304]{1,0:T(8,128)S(1)}, f32[40,4304]{1,0:T(8,128)}, u32[]{:S(2)}, u32[]{:S(2)}) collective-permute-start(f32[40,4304]{1,0:T(8,128)S(1)} %copy-done.13), channel_id=1, source_target_pairs={{0,2},{1,3},{2,4},{3,5},{4,6},{5,7},{6,8},{7,9},{8,10},{9,11},{10,... | collective-permute-start | bytes 2065928
  2344.0 101.6 %collective-permute-start.16 = (f32[40,4304]{1,0:T(8,128)S(1)}, f32[40,4304]{1,0:T(8,128)}, u32[]{:S(2)}, u32[]{:S(2)}) collective-permute-start(f32[40,4304]{1,0:T(8,128)S(1)} %copy-done.13), channel_id=1, source_target_pairs={{0,1},{1,2},{2,3},{3,4},{4,5},{5,6},{6,7},{7,8},{8,9},{9,10},{10,1... | collective-permute-start | bytes 2065928
  2378.5 67.1 %collective-permute-start.19 = (f32[4,4304]{1,0:T(4,128)}, f32[4,4304]{1,0:T(4,128)S(1)}, u32[]{:S(2)}, u32[]{:S(2)}) collective-permute-start(f32[4,4304]{1,0:T(4,128)} %slice.46), channel_id=1, source_target_pairs={{0,4},{1,5},{2,6},{3,7},{4,8},{5,9},{6,10},{7,11},{8,12},{9,13},{1... | collective-permute-start | bytes 206600
  (16 other events, 42.3 us)
Sparse Core Ops, SparseCore 0:
  10.8 80.0 all-gather.9
  93.8 56.0 all-gather.11
  152.6 140.3 all-gather.13
  295.7 97.9 all-gather.15
where the time goes:
time: 2480 us; the launch traced here: 2470 us
  blocking collectives  1720 us (69%)
  waiting for transfers between devices  276 us (11%)
  local copies, waits for them, and re-layouts  229 us (9%)
  starting transfers between devices  104 us (4%)
  matrix products  102 us (4%)
    unnamed x4, blocking collectives  1660 us
    unnamed x116, local copies, waits for them, and re-layouts  146 us
    all_to_all x1, waiting for transfers between devices, local(): lax.all_to_all(projected, 'seq', split_axis=3, concat_axis=1, tiled=True)  111 us
    unnamed x28, waiting for transfers between devices  95.3 us
    unnamed x24, starting transfers between devices  78.1 us
    all_gather x1, blocking collectives, local(): lax.all_gather(qv_bias, ('dp', 'seq'), axis=1, tiled=True)  62.3 us
    all_gather x1, waiting for transfers between devices, local(): lax.all_gather(down_weight, ('dp', 'seq'), axis=1, tiled=True)  51.9 us
  transfers between devices with their start and end apart: 32, of which 9 were waited for; matrix products, arithmetic and copies ran while one was open for 31% of the time, Pallas kernels for 0%

commit v1 on v0

--- a/solution.py
+++ b/solution.py
@@ -8,6 +8,22 @@
 EPS = 1e-06
 GELU_C = 0.7978845608028654
 GELU_A = 0.044715
+
+
+def exchange_in_pairs(x, axis, split, join):
+    ways, here = (lax.axis_size(axis), lax.axis_index(axis))
+    width = x.shape[split] // ways
+    dims = list(x.shape)
+    dims[split] = width
+    height = dims[join]
+    dims[join] = height * ways
+    full = jnp.zeros(dims, x.dtype)
+    for mask in range(ways):
+        part = lax.dynamic_slice_in_dim(x, (here ^ mask) * width, width, axis=split)
+        if mask:
+            part = lax.ppermute(part, axis, [(d, d ^ mask) for d in range(ways)])
+        full = lax.dynamic_update_slice_in_dim(full, part, (here ^ mask) * height, axis=join)
+    return full
 
 
 def layer_norm(values, gain_row, offset):
@@ -163,7 +179,7 @@
         jnp.dot(attn_input, qkv_full, preferred_element_type=jnp.float32) + bias_full
     ).astype(jnp.bfloat16)
     projected = projected.reshape(images, tok_rows, 3, model_width)
-    by_heads = lax.all_to_all(projected, "seq", split_axis=3, concat_axis=1, tiled=True)
+    by_heads = exchange_in_pairs(projected, "seq", 3, 1)
 
     def attend_one(one_image):
         queries = one_image[:, 0].reshape(length, head_share, HEAD)

time: 2480 us -> 2440 us (0.984)
  waiting for transfers between devices: 276 us -> 186 us
  local copies, waits for them, and re-layouts: 229 us -> 287 us
    all_to_all x1 -> x0, waiting for transfers between devices: 111 us -> none  [local(): lax.all_to_all(projected, 'seq', split_axis=3, concat_axis=1, tiled=True)]
    dynamic_update_slice x0 -> x4, local copies, waits for them, and re-layouts: none -> 67.9 us  [exchange_in_pairs(): lax.dynamic_update_slice_in_dim(full, part, (here ^ mask) * height, axis=...]
    unnamed x116 -> x120, local copies, waits for them, and re-layouts: 146 us -> 151 us
  transfers between devices with their start and end apart: 32 -> 34, of which waited for: 9 -> 12; matrix products, arithmetic and copies ran while one was open for 31% -> 34% of each run, Pallas kernels for 0% -> 0%
where the time goes in v1:
time: 2440 us; the launch traced here: 2430 us
  blocking collectives  1720 us (70%)
  local copies, waits for them, and re-layouts  287 us (12%)
  waiting for transfers between devices  186 us (8%)
  matrix products  104 us (4%)
  starting transfers between devices  96.5 us (4%)
    unnamed x4, blocking collectives  1660 us
    unnamed x120, local copies, waits for them, and re-layouts  151 us
    unnamed x28, waiting for transfers between devices  105 us
    unnamed x24, starting transfers between devices  76.2 us
    dynamic_update_slice x4, local copies, waits for them, and re-layouts, exchange_in_pairs(): lax.dynamic_update_slice_in_dim(full, part, (here ^ mask) * height, axis=...  67.9 us
    all_gather x1, blocking collectives, local(): lax.all_gather(qv_bias, ('dp', 'seq'), axis=1, tiled=True)  62.5 us
  transfers between devices with their start and end apart: 34, of which 12 were waited for; matrix products, arithmetic and copies ran while one was open for 34% of the time, Pallas kernels for 0%

profile of v1, /device:TPU:19, one launch (start us, length us, event | category | flops | bytes accessed | tf_op | source)
XLA Modules:
  0.0 2432.1 jit_solution(10180205821874332312)
XLA Ops:
  18.0 41.7 %all-reduce.22 = (bf16[1152]{0:T(1024)(128)(2,1)S(1)}, bf16[1152]{0:T(1024)(128)(2,1)S(1)}, bf16[1152]{0:T(1024)(128)(2,1)}, bf16[1152]{0:T(1024)(128)(2,1)}, bf...) all-reduce(bf16[1152]{0:T(1024)(128)(2,1)S(1)} %dynamic-update-slic, ...), channel_id=1, replica_groups=mesh['dp'=8,'seq'=4] {'dp','seq'}, use_global_device_ids=true, to_apply=%add.1 | all-reduce | flops 6912 | bytes 27648
  59.7 62.5 %all-gather.1 = bf16[32,36,2]{1,2,0:T(2,128)(2,1)S(1)} all-gather(bf16[1,36,2]{1,2,0:T(2,128)(2,1)} %bitcast.192), channel_id=1, replica_groups=mesh['dp'=8,'seq'=4] {'dp','seq'}, dimensions={0}, use_global_device_ids=true | all-gather | bytes 4752 | tf_op jit(solution)/shard_map/all_gather | solution.py:162
  123.8 12.4 reshape.265
  136.2 6.5 fusion.22
  142.8 2.8 reshape.240
  145.6 5.7 constant_dynamic-slice_fusion.5
  152.2 2.6 collective-permute-start
  158.7 17.5 dynamic_update_slice.33
  176.2 6.4 collective-permute-done
  185.0 17.3 dynamic_update_slice.34
  202.4 4.3 collective-permute-done.1
  209.1 15.3 dynamic_update_slice.35
  224.4 9.2 collective-permute-done.2
  236.0 17.7 dynamic_update_slice.36
  253.7 10.4 while.18
  264.1 3.2 copy.85
  267.3 4.2 all-to-all-start
  278.7 5.2 reshape.269
  283.9 6.4 all-to-all-done
  294.7 3.3 fusion.46
  300.0 14.7 reshape.271
  314.6 6.7 convolution_add_fusion
  323.6 9.9 fusion.40
  333.5 37.7 %all-gather.16.cloned.1.call-done = bf16[32,36,4304]{2,1,0:T(8,128)(2,1)} async-done(((bf16[1,36,4304]{2,1,0:T(8,128)(2,1)}), bf16[32,36,4304]{2,1,0:T(8,128)(2,1)}) %all-gather.16.cloned.1.call-update) | async-done | bytes 9916432 | tf_op jit(solution)/shard_map/all_gather | solution.py:208
  371.3 14.4 reshape.273
  385.7 8.8 convert_reduce_fusion
  396.0 8.3 multiply_reduce_fusion.1
  408.0 4.0 copy.88
  412.1 5.0 all-to-all-start.1
  417.1 494.5 %fusion.3 = f32[4304,40]{0,1:T(8,128)} fusion(f32[4304,1152]{0,1:T(8,128)} %fusion.40), kind=kCustom, calls=%all-reduce-scatter.3 | all-reduce-scatter fusion | flops 5509121 | bytes 20521472
  911.6 4.4 collective-permute-start.25
  916.0 4.3 collective-permute-start.24
  922.2 4.9 copy.96
  933.0 23.9 while.19
  956.9 7.1 copy.92
  964.0 7.1 all-to-all-start.2
  971.1 11.3 fusion.39
  982.4 9.9 fusion.30
  995.1 3.9 fusion.34
  999.7 15.6 concatenate.15
  1016.2 17.1 all-to-all-done.2
  1035.4 2.6 copy.94
  1037.9 3.8 reshape.246
  1041.8 7.9 fusion.48
  1049.7 1056.8 %fusion.42 = (f32[48,3456]{1,0:T(8,128)S(1)}, f32[48,1152]{1,0:T(8,128)S(1)}, f32[40,4304]{1,0:T(8,128)}) fusion(f32[1152,3456]{1,0:T(8,128)} %fusion.48, f32[1152,1152]{1,0:T(8,128)} %fusion.34, f32[1152,4304]{1,0:T(8,128)} %fusion.39), kind=kCustom, calls=%all-reduce-scatter.4 | all-reduce-scatter fusion | flops 12587010 | bytes 42639872
  2106.5 4.2 collective-permute-start.17
  2110.8 8.3 fusion.41
  2119.3 4.4 collective-permute-start.16
  2130.5 36.0 %collective-permute-done.18 = f32[36,1152]{1,0:T(8,128)S(1)} collective-permute-done((f32[36,1152]{1,0:T(8,128)S(1)}, f32[36,1152]{1,0:T(8,128)S(1)}, u32[]{:S(2)}, u32[]{:S(2)}) %collective-permute-start.18) | collective-permute-done | bytes 165920
  2171.7 63.4 %all-reduce.21 = (f32[1152]{0:T(1024)}, f32[1152]{0:T(1024)}, f32[2,1152]{1,0:T(2,128)}, f32[1152]{0:T(1024)}, f32[1152]{0:T(1024)}, /*index=5*/f32[1152]{0:T(1024)}, f32[4304]{0:T(1024)}, f32[1152]{0:T(1024)}) all-reduce(f32[1152]{0:T(1024)} %get-tuple-element.153, ...), channel_id=2, replica_groups=mesh['dp'=8,'seq'=4] {'dp','seq'}, use_global_device_ids=true, to_apply=%region_16.17.clone | all-reduce | flops 13520 | bytes 108160
  2235.1 5.7 collective-permute-start.14
  2243.7 6.9 collective-permute-start.12
  2250.6 4.9 collective-permute-start.11
  2256.2 7.6 collective-permute-done.12
  2266.0 3.2 collective-permute-start.6
  2281.7 8.2 collective-permute-start.4
  2291.9 2.7 add_convert_fusion.1
  2294.6 8.8 concatenate.13
  2305.3 2.5 collective-permute-start.20
  2307.8 2.5 collective-permute-start.19
  2311.0 31.4 %collective-permute-done.4 = f32[48,3456]{1,0:T(8,128)} collective-permute-done((f32[48,3456]{1,0:T(8,128)S(1)}, f32[48,3456]{1,0:T(8,128)}, u32[]{:S(2)}, u32[]{:S(2)}) %collective-permute-start.4) | collective-permute-done | bytes 663584
  2344.4 26.5 %collective-permute-done.3 = f32[48,3456]{1,0:T(8,128)} collective-permute-done((f32[48,3456]{1,0:T(8,128)S(1)}, f32[48,3456]{1,0:T(8,128)}, u32[]{:S(2)}, u32[]{:S(2)}) %collective-permute-start.3) | collective-permute-done | bytes 663584
  2370.9 36.8 %concatenate.12 = f32[420,3456]{1,0:T(8,128)} concatenate(f32[36,3456]{1,0:T(8,128)} %collective-permute-done.10, f32[48,3456]{1,0:T(8,128)} %copy-done.22, f32[48,3456]{1,0:T(8,128)} %collective-permute-done.8, f32[48,3456]{1,0:T(8,128)} %collective-permute-done.7, f32[48,3456]{1,0:T(8,128)} %collective-permute-done.6, f32[48,3456]{1,0:T(8,128)} %collective-permute-done.5, ...), dimensions={0} | concatenate | bytes 11612160
  2409.6 14.5 concatenate.14
  (259 shorter events, 133.0 us)
Async XLA Ops:
  7.2 115.2 %copy-start = (bf16[2,144,1152]{2,1,0:T(8,128)(2,1)S(1)}, bf16[2,144,1152]{2,1,0:T(8,128)(2,1)}, u32[]{:S(2)}) copy-start(bf16[2,144,1152]{2,1,0:T(8,128)(2,1)} %param.18) | copy-start | bytes 1990660
  7.2 116.6 %all-gather.10.cloned.1.call-start = ((), (), s32[]{:S(2)}) async-start(), calls=%async_computation.3 | async-start | bytes 9123840 | tf_op jit(solution)/shard_map/all_gather | solution.py:161
  7.9 270.8 %all-gather.12.cloned.1.call-start = ((), (), s32[]{:S(2)}) async-start(), calls=%async_computation.4 | async-start | bytes 3041280 | tf_op jit(solution)/shard_map/all_gather | solution.py:163
  8.7 291.3 %all-gather.14.cloned.1.call-start = ((), (), s32[]{:S(2)}) async-start(), calls=%async_computation.5 | async-start | bytes 11489280 | tf_op jit(solution)/shard_map/all_gather | solution.py:207
  9.4 361.8 %all-gather.16.cloned.1.call-start = ((), (), s32[]{:S(2)}) async-start(), calls=%async_computation.6 | async-start | bytes 11489280 | tf_op jit(solution)/shard_map/all_gather | solution.py:208
  11.3 112.5 %copy-start.39 = (f32[2,144]{1,0:T(2,128)}, f32[2,144]{1,0:T(2,128)S(1)}, u32[]{:S(2)}) copy-start(f32[2,144]{1,0:T(2,128)S(1)} %broadcast_multiply_fusion.5) | copy-start | bytes 3460
  11.4 124.8 %copy-start.41 = (f32[288]{0:T(512)}, f32[288]{0:T(512)S(1)}, u32[]{:S(2)}) copy-start(f32[288]{0:T(512)S(1)} %div.27) | copy-start | bytes 3460
  12.8 111.0 %copy-start.40 = (f32[2,144]{1,0:T(2,128)}, f32[2,144]{1,0:T(2,128)S(1)}, u32[]{:S(2)}) copy-start(f32[2,144]{1,0:T(2,128)S(1)} %add_rsqrt_fusion.1) | copy-start | bytes 3460
  12.9 123.3 %copy-start.43 = (f32[288]{0:T(512)}, f32[288]{0:T(512)S(1)}, u32[]{:S(2)}) copy-start(f32[288]{0:T(512)S(1)} %rsqrt.21) | copy-start | bytes 3460
  59.7 76.5 %copy-start.38 = (f32[1152]{0:T(1024)}, f32[1152]{0:T(1024)S(1)}, u32[]{:S(2)}) copy-start(f32[1152]{0:T(1024)S(1)} %convert_element_type.138) | copy-start | bytes 13828
  59.7 76.5 %copy-start.32 = (f32[1152]{0:T(1024)}, f32[1152]{0:T(1024)S(1)}, u32[]{:S(2)}) copy-start(f32[1152]{0:T(1024)S(1)} %convert_element_type.137) | copy-start | bytes 13828
  152.2 30.4 %collective-permute-start = (bf16[2,144,3,288]{3,1,2,0:T(8,128)(2,1)}, bf16[2,144,3,288]{3,1,2,0:T(8,128)(2,1)}, u32[]{:S(2)}, u32[]{:S(2)}) collective-permute-start(bf16[2,144,3,288]{3,1,2,0:T(8,128)(2,1)} %copy.79), channel_id=1, source_target_pairs={{0,1},{1,0},{2,3},{3,2},{4,5},{5,4},{6,7},{7,6},{8,9},{9,8},{10,11... | collective-permute-start | bytes 1493000 | tf_op jit(solution)/shard_map/ppermute | solution.py:24
  155.8 50.9 %collective-permute-start.1 = (bf16[2,144,3,288]{3,1,2,0:T(8,128)(2,1)}, bf16[2,144,3,288]{3,1,2,0:T(8,128)(2,1)}, u32[]{:S(2)}, u32[]{:S(2)}) collective-permute-start(bf16[2,144,3,288]{3,1,2,0:T(8,128)(2,1)} %copy.81), channel_id=1, source_target_pairs={{0,2},{1,3},{2,0},{3,1},{4,6},{5,7},{6,4},{7,5},{8,10},{9,11},{10,... | collective-permute-start | bytes 1493000 | tf_op jit(solution)/shard_map/ppermute | solution.py:24
  155.8 77.8 %collective-permute-start.2 = (bf16[2,144,3,288]{3,1,2,0:T(8,128)(2,1)S(1)}, bf16[2,144,3,288]{3,1,2,0:T(8,128)(2,1)}, u32[]{:S(2)}, u32[]{:S(2)}) collective-permute-start(bf16[2,144,3,288]{3,1,2,0:T(8,128)(2,1)S(1)} %copy.83), channel_id=1, source_target_pairs={{0,3},{1,2},{2,1},{3,0},{4,7},{5,6},{6,5},{7,4},{8,11},{9,10},{10,... | collective-permute-start | bytes 1493000 | tf_op jit(solution)/shard_map/ppermute | solution.py:24
  264.1 12.0 copy-start.13
  267.3 22.9 all-to-all-start
  300.0 14.7 copy-start.5
  314.6 9.0 copy-start.14
  385.7 10.3 copy-start.30
  385.7 10.3 copy-start.35
  396.0 8.3 copy-start.6
  396.0 8.3 copy-start.15
  405.4 589.7 %copy-start.2 = (f32[288,1152]{1,0:T(8,128)}, f32[288,1152]{1,0:T(8,128)S(1)}, u32[]{:S(2)}) copy-start(f32[288,1152]{1,0:T(8,128)S(1)} %get-tuple-element.201) | copy-start | bytes 3981316
  412.1 510.1 %all-to-all-start.1 = ((bf16[2,144,1152]{1,0,2:T(2,128)(2,1)}), bf16[2,144,1152]{1,0,2:T(2,128)(2,1)}, u32[]{:S(2)}, u32[]{:S(2)}) async-start(bf16[2,144,1152]{1,0,2:T(2,128)(2,1)} %copy.88), calls=%async_computation.1 | async-start | bytes 2359296 | tf_op jit(solution)/shard_map/all_to_all | solution.py:266
  911.6 87.5 %collective-permute-start.25 = (f32[4304,40]{0,1:T(8,128)}, f32[4304,40]{0,1:T(8,128)}, u32[]{:S(2)}, u32[]{:S(2)}) collective-permute-start(f32[4304,40]{0,1:T(8,128)} %fusion.3), channel_id=1, source_target_pairs={{0,3},{1,4},{2,5},{3,6},{4,7},{5,8},{6,9},{7,10},{8,11},{9,12},{10... | collective-permute-start | bytes 2065928
  916.0 83.1 %collective-permute-start.24 = (f32[4304,40]{0,1:T(8,128)}, f32[4304,40]{0,1:T(8,128)}, u32[]{:S(2)}, u32[]{:S(2)}) collective-permute-start(f32[4304,40]{0,1:T(8,128)} %fusion.3), channel_id=1, source_target_pairs={{0,2},{1,3},{2,4},{3,5},{4,6},{5,7},{6,8},{7,9},{8,10},{9,11},{10,... | collective-permute-start | bytes 2065928
  920.3 79.4 %collective-permute-start.23 = (f32[4304,40]{0,1:T(8,128)}, f32[4304,40]{0,1:T(8,128)}, u32[]{:S(2)}, u32[]{:S(2)}) collective-permute-start(f32[4304,40]{0,1:T(8,128)} %fusion.3), channel_id=1, source_target_pairs={{0,1},{1,2},{2,3},{3,4},{4,5},{5,6},{6,7},{7,8},{8,9},{9,10},{10,1... | collective-permute-start | bytes 2065928
  963.9 7.1 copy-start.36
  964.0 69.3 %all-to-all-start.2 = ((bf16[2,576,3,288]{3,0,2,1:T(2,128)(2,1)}), bf16[2,576,3,288]{3,0,2,1:T(2,128)(2,1)}, u32[]{:S(2)}, u32[]{:S(2)}) async-start(bf16[2,576,3,288]{3,0,2,1:T(2,128)(2,1)} %copy.92), calls=%async_computation.2 | async-start | bytes 5308416 | tf_op jit(solution)/shard_map/all_to_all | solution.py:288
  971.0 11.3 copy-start.45
  982.4 12.7 copy-start.17
  993.2 5.9 collective-permute-start.26
  1049.6 1061.1 %copy-start.1 = (bf16[2,144,1152]{2,1,0:T(8,128)(2,1)S(1)}, bf16[2,144,1152]{2,1,0:T(8,128)(2,1)}, u32[]{:S(2)}) copy-start(bf16[2,144,1152]{2,1,0:T(8,128)(2,1)} %param.18) | copy-start | bytes 1990660
  1049.7 1061.1 %copy-start.33 = (f32[1152]{0:T(1024)S(1)}, f32[1152]{0:T(1024)}, u32[]{:S(2)}) copy-start(f32[1152]{0:T(1024)} %copy-done.32) | copy-start | bytes 13828
  1049.7 1061.1 %copy-start.42 = (f32[288]{0:T(512)S(1)}, f32[288]{0:T(512)}, u32[]{:S(2)}) copy-start(f32[288]{0:T(512)} %copy-done.41) | copy-start | bytes 3460
  1049.7 1061.1 %copy-start.44 = (f32[288]{0:T(512)S(1)}, f32[288]{0:T(512)}, u32[]{:S(2)}) copy-start(f32[288]{0:T(512)} %copy-done.43) | copy-start | bytes 3460
  2106.5 62.0 %collective-permute-start.17 = (f32[48,1152]{1,0:T(8,128)S(1)}, f32[48,1152]{1,0:T(8,128)S(1)}, u32[]{:S(2)}, u32[]{:S(2)}) collective-permute-start(f32[48,1152]{1,0:T(8,128)S(1)} %get-tuple-element.196), channel_id=1, source_target_pairs={{0,7},{1,8},{2,9},{3,10},{4,11},{5,12},{6,13},{7,14},{8,15},{9,16}... | collective-permute-start | bytes 663560
  2119.3 52.4 %copy-start.37 = (f32[1152]{0:T(1024)S(1)}, f32[1152]{0:T(1024)}, u32[]{:S(2)}) copy-start(f32[1152]{0:T(1024)} %convert_reduce_fusion.1) | copy-start | bytes 13828
  2119.3 172.6 %copy-start.3 = (f32[288,1152]{1,0:T(8,128)S(1)}, f32[288,1152]{1,0:T(8,128)}, u32[]{:S(2)}) copy-start(f32[288,1152]{1,0:T(8,128)} %copy-done.2) | copy-start | bytes 3981316
  2119.3 115.7 %collective-permute-start.16 = (f32[48,1152]{1,0:T(8,128)S(1)}, f32[48,1152]{1,0:T(8,128)}, u32[]{:S(2)}, u32[]{:S(2)}) collective-permute-start(f32[48,1152]{1,0:T(8,128)S(1)} %get-tuple-element.196), channel_id=1, source_target_pairs={{0,6},{1,7},{2,8},{3,9},{4,10},{5,11},{6,12},{7,13},{8,14},{9,15},... | collective-permute-start | bytes 663560
  2123.7 117.1 %collective-permute-start.15 = (f32[48,1152]{1,0:T(8,128)S(1)}, f32[48,1152]{1,0:T(8,128)}, u32[]{:S(2)}, u32[]{:S(2)}) collective-permute-start(f32[48,1152]{1,0:T(8,128)S(1)} %get-tuple-element.196), channel_id=1, source_target_pairs={{0,5},{1,6},{2,7},{3,8},{4,9},{5,10},{6,11},{7,12},{8,13},{9,14},{... | collective-permute-start | bytes 663560
  2126.5 155.2 %collective-permute-start.9 = (f32[48,3456]{1,0:T(8,128)S(1)}, f32[48,3456]{1,0:T(8,128)S(1)}, u32[]{:S(2)}, u32[]{:S(2)}) collective-permute-start(f32[48,3456]{1,0:T(8,128)S(1)} %get-tuple-element.195), channel_id=1, source_target_pairs={{0,7},{1,8},{2,9},{3,10},{4,11},{5,12},{6,13},{7,14},{8,15},{9,16}... | collective-permute-start | bytes 1990664
  2128.4 38.1 %collective-permute-start.18 = (f32[36,1152]{1,0:T(8,128)S(1)}, f32[36,1152]{1,0:T(8,128)S(1)}, u32[]{:S(2)}, u32[]{:S(2)}) collective-permute-start(f32[36,1152]{1,0:T(8,128)S(1)} %slice.45), channel_id=1, source_target_pairs={{0,8},{1,9},{2,10},{3,11},{4,12},{5,13},{6,14},{7,15},{8,16},{9,17... | collective-permute-start | bytes 497672
  2166.5 123.4 %collective-permute-start.8 = (f32[48,3456]{1,0:T(8,128)S(1)}, f32[48,3456]{1,0:T(8,128)}, u32[]{:S(2)}, u32[]{:S(2)}) collective-permute-start(f32[48,3456]{1,0:T(8,128)S(1)} %get-tuple-element.195), channel_id=1, source_target_pairs={{0,6},{1,7},{2,8},{3,9},{4,10},{5,11},{6,12},{7,13},{8,14},{9,15},... | collective-permute-start | bytes 1990664
  2169.2 100.1 %collective-permute-start.10 = (f32[36,3456]{1,0:T(8,128)}, f32[36,3456]{1,0:T(8,128)}, u32[]{:S(2)}, u32[]{:S(2)}) collective-permute-start(f32[36,3456]{1,0:T(8,128)} %slice.44), channel_id=1, source_target_pairs={{0,8},{1,9},{2,10},{3,11},{4,12},{5,13},{6,14},{7,15},{8,16},{9,17... | collective-permute-start | bytes 1493000
  2235.1 8.6 collective-permute-start.14
  2240.8 9.8 collective-permute-start.13
  2243.7 46.2 %copy-start.24 = (f32[48,1152]{1,0:T(8,128)}, f32[48,1152]{1,0:T(8,128)S(1)}, u32[]{:S(2)}) copy-start(f32[48,1152]{1,0:T(8,128)S(1)} %collective-permute-done.14) | copy-start | bytes 663556
  2243.7 20.1 collective-permute-start.12
  2250.6 41.3 %copy-start.25 = (f32[48,1152]{1,0:T(8,128)}, f32[48,1152]{1,0:T(8,128)S(1)}, u32[]{:S(2)}) copy-start(f32[48,1152]{1,0:T(8,128)S(1)} %collective-permute-done.13) | copy-start | bytes 663556
  2250.6 15.4 collective-permute-start.11
  2263.8 28.1 %copy-start.26 = (f32[48,1152]{1,0:T(8,128)}, f32[48,1152]{1,0:T(8,128)S(1)}, u32[]{:S(2)}) copy-start(f32[48,1152]{1,0:T(8,128)S(1)} %collective-permute-done.12) | copy-start | bytes 663556
  2263.8 39.5 %collective-permute-start.7 = (f32[48,3456]{1,0:T(8,128)S(1)}, f32[48,3456]{1,0:T(8,128)}, u32[]{:S(2)}, u32[]{:S(2)}) collective-permute-start(f32[48,3456]{1,0:T(8,128)S(1)} %get-tuple-element.195), channel_id=1, source_target_pairs={{0,5},{1,6},{2,7},{3,8},{4,9},{5,10},{6,11},{7,12},{8,13},{9,14},{... | collective-permute-start | bytes 1990664
  2266.0 25.8 %copy-start.27 = (f32[48,1152]{1,0:T(8,128)}, f32[48,1152]{1,0:T(8,128)S(1)}, u32[]{:S(2)}) copy-start(f32[48,1152]{1,0:T(8,128)S(1)} %collective-permute-done.11) | copy-start | bytes 663556
  2266.0 39.3 %collective-permute-start.6 = (f32[48,3456]{1,0:T(8,128)S(1)}, f32[48,3456]{1,0:T(8,128)}, u32[]{:S(2)}, u32[]{:S(2)}) collective-permute-start(f32[48,3456]{1,0:T(8,128)S(1)} %get-tuple-element.195), channel_id=1, source_target_pairs={{0,4},{1,5},{2,6},{3,7},{4,8},{5,9},{6,10},{7,11},{8,12},{9,13},{1... | collective-permute-start | bytes 1990664
  2269.2 38.6 %collective-permute-start.5 = (f32[48,3456]{1,0:T(8,128)S(1)}, f32[48,3456]{1,0:T(8,128)}, u32[]{:S(2)}, u32[]{:S(2)}) collective-permute-start(f32[48,3456]{1,0:T(8,128)S(1)} %get-tuple-element.195), channel_id=1, source_target_pairs={{0,3},{1,4},{2,5},{3,6},{4,7},{5,8},{6,9},{7,10},{8,11},{9,12},{10... | collective-permute-start | bytes 1990664
  2281.7 10.2 copy-start.22
  2281.7 60.7 %collective-permute-start.4 = (f32[48,3456]{1,0:T(8,128)S(1)}, f32[48,3456]{1,0:T(8,128)}, u32[]{:S(2)}, u32[]{:S(2)}) collective-permute-start(f32[48,3456]{1,0:T(8,128)S(1)} %get-tuple-element.195), channel_id=1, source_target_pairs={{0,2},{1,3},{2,4},{3,5},{4,6},{5,7},{6,8},{7,9},{8,10},{9,11},{10,... | collective-permute-start | bytes 1990664
  2289.9 81.0 %collective-permute-start.3 = (f32[48,3456]{1,0:T(8,128)S(1)}, f32[48,3456]{1,0:T(8,128)}, u32[]{:S(2)}, u32[]{:S(2)}) collective-permute-start(f32[48,3456]{1,0:T(8,128)S(1)} %get-tuple-element.195), channel_id=1, source_target_pairs={{0,1},{1,2},{2,3},{3,4},{4,5},{5,6},{6,7},{7,8},{8,9},{9,10},{10,1... | collective-permute-start | bytes 1990664
  2294.6 8.8 copy-start.19
  2303.4 106.2 %collective-permute-start.21 = (f32[40,4304]{1,0:T(8,128)S(1)}, f32[40,4304]{1,0:T(8,128)}, u32[]{:S(2)}, u32[]{:S(2)}) collective-permute-start(f32[40,4304]{1,0:T(8,128)S(1)} %copy-done.19), channel_id=1, source_target_pairs={{0,3},{1,4},{2,5},{3,6},{4,7},{5,8},{6,9},{7,10},{8,11},{9,12},{10... | collective-permute-start | bytes 2065928
  2305.3 104.3 %collective-permute-start.20 = (f32[40,4304]{1,0:T(8,128)S(1)}, f32[40,4304]{1,0:T(8,128)}, u32[]{:S(2)}, u32[]{:S(2)}) collective-permute-start(f32[40,4304]{1,0:T(8,128)S(1)} %copy-done.19), channel_id=1, source_target_pairs={{0,2},{1,3},{2,4},{3,5},{4,6},{5,7},{6,8},{7,9},{8,10},{9,11},{10,... | collective-permute-start | bytes 2065928
  2307.8 101.8 %collective-permute-start.19 = (f32[40,4304]{1,0:T(8,128)S(1)}, f32[40,4304]{1,0:T(8,128)}, u32[]{:S(2)}, u32[]{:S(2)}) collective-permute-start(f32[40,4304]{1,0:T(8,128)S(1)} %copy-done.19), channel_id=1, source_target_pairs={{0,1},{1,2},{2,3},{3,4},{4,5},{5,6},{6,7},{7,8},{8,9},{9,10},{10,1... | collective-permute-start | bytes 2065928
  2342.4 67.2 %collective-permute-start.22 = (f32[4,4304]{1,0:T(4,128)}, f32[4,4304]{1,0:T(4,128)S(1)}, u32[]{:S(2)}, u32[]{:S(2)}) collective-permute-start(f32[4,4304]{1,0:T(4,128)} %slice.46), channel_id=1, source_target_pairs={{0,4},{1,5},{2,6},{3,7},{4,8},{5,9},{6,10},{7,11},{8,12},{9,13},{1... | collective-permute-start | bytes 206600
  (20 other events, 46.1 us)
Sparse Core Ops, SparseCore 0:
  10.8 80.0 all-gather.9
  93.7 55.9 all-gather.11
  152.6 126.0 all-gather.13
  281.4 89.8 all-gather.15
